TPU v7x, 512 devices: a whole 4x4x16 slice. The times are simulated.
512 devices in a mesh: docs: 64 (over x, z_lo, core), blk: 8 (over y, z_hi).
Axes of the slice: x: 4, y: 4, z: 16 (z_hi: 2, z_lo: 8; z = z_hi * 8 + z_lo), core: 2. Of those that a mesh axis runs over, the one named last changes fastest.
Arguments:
- group_rows: bfloat16 [8, 16384, 2048], P('blk', 'docs'), may hold values from -0.14941406 to 0.14941406
- group_owner: int32 [8, 16384, 1], P('blk', 'docs'), may hold values from 0 to 63; in each aligned block of 256 rows (0 to 255, 256 to 511, ..., all dimensions but the last counted through in order) at most 8 rows name the same one
- group_doc: int32 [8, 16384], P('blk', 'docs'), may hold values from 0 to 255
- doc_weight: float32 [8, 16384], P('blk', 'docs'), may hold values from 0.1 to 1
- queries: bfloat16 [256, 2048], P('blk'), may hold values from -6 to 6
- precond: bfloat16 [2048, 2048], P(None, 'docs'), may hold values from -0.125 to 0.125
Outputs:
- scores: float32 [256, 8, 16384], P(None, 'blk', 'docs')
Inputs may be any that keep to these rules, and one draw needn't show every extreme that they name: `group_owner`: within the rows of one device, at most 8 groups name the same owner, and some owner gets exactly 8.
All inputs are finite; a program needn't handle non-finite values.
Results may differ from a plain program's by a relative error of at most 0.006.
Values may be sent and summed in bfloat16 or wider, within the bound.
A program may use at most 64 MiB of HBM per device.

v0:
```python
import jax
import jax.numpy as jnp
from jax import lax
from jax.sharding import PartitionSpec as P

NT = (((1,), (1,)), ((), ()))


def shards(group_rows, group_owner, group_doc, doc_weight, queries, precond):
    rows = group_rows[0]
    owner = group_owner[0, :, 0]
    doc_index = group_doc[0]
    peers = lax.axis_size("docs")
    count = rows.shape[0]
    capacity = 2 * count // peers
    slots = peers * capacity
    peer_ids = jnp.arange(peers, dtype=jnp.int32)
    owner_table = peer_ids[:, None] == owner[None, :]
    order = jnp.arange(count, dtype=jnp.int32)
    before = (order[:, None] < order[None, :]).astype(jnp.bfloat16)
    earlier = jnp.dot(owner_table.astype(jnp.bfloat16), before, preferred_element_type=jnp.float32)
    rank = jnp.sum(jnp.where(owner_table, earlier, 0.0), axis=0).astype(jnp.int32)
    slot = owner * capacity + rank
    pick = jnp.arange(slots, dtype=jnp.int32)[:, None] == slot[None, :]
    send_ids = jnp.max(jnp.where(pick, doc_index[None, :], -1), axis=1).reshape(peers, capacity)
    got_ids = lax.all_to_all(send_ids, "docs", split_axis=0, concat_axis=0, tiled=True).reshape(
        slots
    )
    query_pre = jnp.dot(queries, precond, preferred_element_type=jnp.float32).astype(jnp.bfloat16)
    full_rows = lax.all_gather(query_pre, "docs", axis=1, tiled=True)
    full = lax.all_gather(full_rows, "blk", axis=0, tiled=True)
    part = lax.dot_general(rows, full, NT, preferred_element_type=jnp.float32).astype(jnp.bfloat16)
    send = jnp.dot(pick.astype(jnp.bfloat16), part, preferred_element_type=jnp.float32).astype(
        jnp.bfloat16
    )
    send = send.reshape(peers, capacity, send.shape[1])
    got = lax.all_to_all(send, "docs", split_axis=0, concat_axis=0, tiled=True)
    got = got.reshape(slots, got.shape[2])
    doc_ids = jnp.arange(doc_weight.shape[1], dtype=jnp.int32)
    member = (got_ids[:, None] == doc_ids[None, :]).astype(jnp.bfloat16)
    scores = lax.dot_general(
        got, member, (((0,), (0,)), ((), ())), preferred_element_type=jnp.float32
    )
    return (scores * doc_weight[0][None, :])[:, None, :]


def solution(mesh):
    return jax.shard_map(
        shards,
        mesh=mesh,
        in_specs=(
            P("blk", "docs", None),
            P("blk", "docs", None),
            P("blk", "docs"),
            P("blk", "docs"),
            P("blk", None),
            P(None, "docs"),
        ),
        out_specs=P(None, "blk", "docs"),
        check_vma=False,
    )
```

profile of v0, /device:TPU:1, one launch (start us, length us, event | category | flops | bytes accessed | tf_op | source)
XLA Modules:
  0.0 259.1 jit_solution(14440110676353129902)
XLA Ops:
  6.5 0.0 copy-start
  6.5 0.0 all-gather.2.cloned.1.call-start
  6.5 1.2 convolution_convert_fusion.2
  7.7 0.1 copy.16
  7.8 129.0 %all_gather.6 = bf16[32,2048]{0,1:T(8,128)(2,1)S(1)} all-gather(bf16[32,32]{0,1:T(8,128)(2,1)S(1)} %copy.16), channel_id=1, replica_groups=mesh['docs'=64,'blk'=8] {'docs'}, dimensions={1}, use_global_device_ids=true | all-gather | bytes 133120 | tf_op jit(solution)/shard_map/all_gather | solution.py:30
  136.8 0.8 copy.17
  137.6 0.0 all-gather.2.cloned.1.call-update
  137.7 0.0 copy-start.1
  137.7 0.7 copy-done.1
  138.4 0.2 fusion.2
  138.5 0.0 copy-start.2
  138.6 0.7 copy-done.2
  139.2 0.1 select_reduce_fusion
  139.4 0.7 all_to_all.10
  140.1 4.2 %all-to-all-start.1 = ((s32[64,1,8]{2,1,0:T(1,128)}), s32[64,1,8]{2,1,0:T(1,128)S(1)}, u32[]{:S(2)}, u32[]{:S(2)}) async-start(s32[64,1,8]{2,1,0:T(1,128)} %bitcast.5), calls=%async_computation.1 | async-start | bytes 65536 | tf_op jit(solution)/shard_map/all_to_all | solution.py:26
  144.3 77.4 %all-gather.2.cloned.1.call-done = bf16[256,2048]{1,0:T(8,128)(2,1)} async-done(((bf16[32,2048]{1,0:T(8,128)(2,1)}), bf16[256,2048]{1,0:T(8,128)(2,1)}) %all-gather.2.cloned.1.call-update) | async-done | bytes 1048592 | tf_op jit(solution)/shard_map/all_gather | solution.py:31
  221.7 0.0 copy-done
  221.7 2.7 %fusion.1 = bf16[64,8,256]{2,1,0:T(8,128)(2,1)} fusion(bf16[256,2048]{1,0:T(8,128)(2,1)} %all-gather.2.cloned.1.call-done, bf16[1,256,2048]{2,1,0:T(8,128)(2,1)S(1)} %copy-done, s32[256]{0:T(256)S(1)} %convert_add_fusion), kind=kOutput, calls=%fused_computation.3 | convolution fusion | flops 335872000 | bytes 2360320 | tf_op jit(solution)/shard_map/dot_general | solution.py:33
  224.4 0.0 all-to-all-done.1
  224.4 7.2 %all-to-all-start = ((bf16[64,8,256]{2,1,0:T(8,128)(2,1)}), bf16[64,8,256]{2,1,0:T(8,128)(2,1)S(1)}, u32[]{:S(2)}, u32[]{:S(2)}) async-start(bf16[64,8,256]{2,1,0:T(8,128)(2,1)} %fusion.1), calls=%async_computation | async-start | bytes 524288 | tf_op jit(solution)/shard_map/all_to_all | solution.py:37
  231.6 0.6 broadcast.7
  232.2 0.7 reduce.3
  232.9 0.1 eq.47
  233.0 0.0 copy-start.3
  233.0 17.9 %all-to-all-done = bf16[64,8,256]{2,1,0:T(8,128)(2,1)S(1)} async-done(((bf16[64,8,256]{2,1,0:T(8,128)(2,1)}), bf16[64,8,256]{2,1,0:T(8,128)(2,1)S(1)}, u32[]{:S(2)}, u32[]{:S(2)}) %all-to-all-start) | async-done | bytes 262176 | tf_op jit(solution)/shard_map/all_to_all | solution.py:37
  250.9 0.0 copy-done.3
  250.9 0.3 fusion
  251.2 1.0 copy.19
  (1 shorter events, 0.0 us)
Async XLA Ops:
  6.5 215.1 %copy-start = (bf16[1,256,2048]{2,1,0:T(8,128)(2,1)S(1)}, bf16[1,256,2048]{2,1,0:T(8,128)(2,1)}, u32[]{:S(2)}) copy-start(bf16[1,256,2048]{2,1,0:T(8,128)(2,1)} %param.6) | copy-start | bytes 3145732
  6.5 215.1 %all-gather.2.cloned.1.call-start = ((), (), s32[]{:S(2)}) async-start(), calls=%async_computation.2 | async-start | bytes 1179648 | tf_op jit(solution)/shard_map/all_gather | solution.py:31
  137.7 0.7 copy-start.1
  138.5 0.7 copy-start.2
  140.1 84.3 %all-to-all-start.1 = ((s32[64,1,8]{2,1,0:T(1,128)}), s32[64,1,8]{2,1,0:T(1,128)S(1)}, u32[]{:S(2)}, u32[]{:S(2)}) async-start(s32[64,1,8]{2,1,0:T(1,128)} %bitcast.5), calls=%async_computation.1 | async-start | bytes 65536 | tf_op jit(solution)/shard_map/all_to_all | solution.py:26
  224.4 26.5 %all-to-all-start = ((bf16[64,8,256]{2,1,0:T(8,128)(2,1)}), bf16[64,8,256]{2,1,0:T(8,128)(2,1)S(1)}, u32[]{:S(2)}, u32[]{:S(2)}) async-start(bf16[64,8,256]{2,1,0:T(8,128)(2,1)} %fusion.1), calls=%async_computation | async-start | bytes 524288 | tf_op jit(solution)/shard_map/all_to_all | solution.py:37
  233.0 17.9 %copy-start.3 = (f32[1,256]{1,0:T(1,128)S(1)}, f32[1,256]{1,0:T(1,128)}, u32[]{:S(2)}) copy-start(f32[1,256]{1,0:T(1,128)} %param.9) | copy-start | bytes 3076
Sparse Core Ops, SparseCore 0:
  137.8 83.8 all-gather.1
where the time goes:
time: 259 us
  blocking collectives  129 us (50%)
  waiting for transfers between devices  95.3 us (37%)
  between operations  13.5 us (5%)
  starting transfers between devices  11.4 us (4%)
  local copies, waits for them, and re-layouts  4.65 us (2%)
  matrix products  4.45 us (2%)
    all_gather x1, blocking collectives, shards(): full_rows = lax.all_gather(query_pre, 'docs', axis=1, tiled=True)  129 us
    all_gather x1, waiting for transfers between devices, shards(): full = lax.all_gather(full_rows, 'blk', axis=0, tiled=True)  77.4 us
    all_to_all x1, waiting for transfers between devices, shards(): got = lax.all_to_all(send, 'docs', split_axis=0, concat_axis=0, tiled=True)  17.9 us
    all_to_all x1, starting transfers between devices, shards(): got = lax.all_to_all(send, 'docs', split_axis=0, concat_axis=0, tiled=True)  7.2 us
  transfers between devices with their start and end apart: 3, of which 2 were waited for; matrix products, arithmetic and copies ran while one was open for 2% of the time, Pallas kernels for 0%

commit v1 on v0

--- a/solution.py
+++ b/solution.py
@@ -27,7 +27,8 @@
         slots
     )
     query_pre = jnp.dot(queries, precond, preferred_element_type=jnp.float32).astype(jnp.bfloat16)
-    full_rows = lax.all_gather(query_pre, "docs", axis=1, tiled=True)
+    repeated = jnp.stack([query_pre] * lax.axis_size("docs"))
+    full_rows = jnp.concatenate(lax.all_to_all(repeated, "docs", 0, 0), axis=1)
     full = lax.all_gather(full_rows, "blk", axis=0, tiled=True)
     part = lax.dot_general(rows, full, NT, preferred_element_type=jnp.float32).astype(jnp.bfloat16)
     send = jnp.dot(pick.astype(jnp.bfloat16), part, preferred_element_type=jnp.float32).astype(

time: 259 us -> 164 us (0.63)
  blocking collectives: 129 us -> 31.4 us
    all_gather x1 -> x0, blocking collectives: 129 us -> none  [shards(): full_rows = lax.all_gather(query_pre, 'docs', axis=1, tiled=True)]
    all_to_all x0 -> x1, blocking collectives: none -> 31.4 us  [shards(): full_rows = jnp.concatenate(lax.all_to_all(repeated, 'docs', 0, 0), axis=1)]
  transfers between devices with their start and end apart: 3 -> 3, of which waited for: 2 -> 2; matrix products, arithmetic and copies ran while one was open for 2% -> 3% of each run, Pallas kernels for 0% -> 0%
where the time goes in v1:
time: 164 us
  waiting for transfers between devices  94.1 us (57%)
  blocking collectives  31.4 us (19%)
  between operations  13.5 us (8%)
  starting transfers between devices  13.3 us (8%)
  local copies, waits for them, and re-layouts  5.89 us (4%)
  matrix products  4.46 us (3%)
    all_gather x1, waiting for transfers between devices, shards(): full = lax.all_gather(full_rows, 'blk', axis=0, tiled=True)  76.2 us
    all_to_all x1, blocking collectives, shards(): full_rows = jnp.concatenate(lax.all_to_all(repeated, 'docs', 0, 0), axis=1)  31.4 us
    all_to_all x1, waiting for transfers between devices, shards(): got = lax.all_to_all(send, 'docs', split_axis=0, concat_axis=0, tiled=True)  17.9 us
    all_to_all x1, starting transfers between devices, shards(): got = lax.all_to_all(send, 'docs', split_axis=0, concat_axis=0, tiled=True)  7.19 us
    all_to_all x1, starting transfers between devices, shards(): lax.all_to_all(send_ids, 'docs', split_axis=0, concat_axis=0, tiled=True)  6.06 us
  transfers between devices with their start and end apart: 3, of which 2 were waited for; matrix products, arithmetic and copies ran while one was open for 3% of the time, Pallas kernels for 0%

profile of v1, /device:TPU:1, one launch (start us, length us, event | category | flops | bytes accessed | tf_op | source)
XLA Modules:
  0.0 163.5 jit_solution(14101425384419733864)
XLA Ops:
  6.5 0.0 copy-start
  6.5 0.0 all-gather.2.cloned.1.call-start
  6.5 1.2 convolution_convert_fusion.2
  7.7 0.1 stack.2
  7.8 0.4 reshape.43
  8.3 31.4 %all_to_all.19 = bf16[64,2,512]{2,1,0:T(2,128)(2,1)S(1)} all-to-all(bf16[64,2,512]{2,1,0:T(2,128)(2,1)S(1)} %reshape.43), channel_id=1, replica_groups=mesh['docs'=64,'blk'=8] {'docs'}, dimensions={0} | all-to-all | bytes 262144 | tf_op jit(solution)/shard_map/all_to_all | solution.py:31
  39.7 0.3 reshape.44
  40.0 0.2 copy.12
  40.2 1.2 reshape.31
  41.4 0.0 all-gather.2.cloned.1.call-update
  41.4 0.0 copy-start.1
  41.4 0.7 copy-done.1
  42.1 0.2 fusion.2
  42.3 0.0 copy-start.2
  42.3 0.7 copy-done.2
  43.0 0.1 select_reduce_fusion
  43.1 0.7 all_to_all.14
  43.8 6.1 %all-to-all-start.2 = ((s32[64,1,8]{2,1,0:T(1,128)}), s32[64,1,8]{2,1,0:T(1,128)S(1)}, u32[]{:S(2)}, u32[]{:S(2)}) async-start(s32[64,1,8]{2,1,0:T(1,128)} %bitcast.6), calls=%async_computation.2 | async-start | bytes 65536 | tf_op jit(solution)/shard_map/all_to_all | solution.py:26
  49.9 76.2 %all-gather.2.cloned.1.call-done = bf16[256,2048]{1,0:T(8,128)(2,1)} async-done(((bf16[32,2048]{1,0:T(8,128)(2,1)}), bf16[256,2048]{1,0:T(8,128)(2,1)}) %all-gather.2.cloned.1.call-update) | async-done | bytes 1048592 | tf_op jit(solution)/shard_map/all_gather | solution.py:32
  126.1 0.0 copy-done
  126.1 2.7 %fusion.1 = bf16[64,8,256]{2,1,0:T(8,128)(2,1)} fusion(bf16[256,2048]{1,0:T(8,128)(2,1)} %all-gather.2.cloned.1.call-done, bf16[1,256,2048]{2,1,0:T(8,128)(2,1)S(1)} %copy-done, s32[256]{0:T(256)S(1)} %convert_add_fusion), kind=kOutput, calls=%fused_computation.3 | convolution fusion | flops 335872000 | bytes 2360320 | tf_op jit(solution)/shard_map/dot_general | solution.py:34
  128.8 0.0 all-to-all-done.2
  128.8 7.2 %all-to-all-start.1 = ((bf16[64,8,256]{2,1,0:T(8,128)(2,1)}), bf16[64,8,256]{2,1,0:T(8,128)(2,1)S(1)}, u32[]{:S(2)}, u32[]{:S(2)}) async-start(bf16[64,8,256]{2,1,0:T(8,128)(2,1)} %fusion.1), calls=%async_computation.1 | async-start | bytes 524288 | tf_op jit(solution)/shard_map/all_to_all | solution.py:38
  136.0 0.6 broadcast.9
  136.6 0.7 reduce.3
  137.3 0.1 eq.47
  137.4 0.0 copy-start.3
  137.4 17.9 %all-to-all-done.1 = bf16[64,8,256]{2,1,0:T(8,128)(2,1)S(1)} async-done(((bf16[64,8,256]{2,1,0:T(8,128)(2,1)}), bf16[64,8,256]{2,1,0:T(8,128)(2,1)S(1)}, u32[]{:S(2)}, u32[]{:S(2)}) %all-to-all-start.1) | async-done | bytes 262176 | tf_op jit(solution)/shard_map/all_to_all | solution.py:38
  155.3 0.0 copy-done.3
  155.3 0.3 fusion
  155.7 1.0 copy.14
  (1 shorter events, 0.0 us)
Async XLA Ops:
  6.5 119.6 %copy-start = (bf16[1,256,2048]{2,1,0:T(8,128)(2,1)S(1)}, bf16[1,256,2048]{2,1,0:T(8,128)(2,1)}, u32[]{:S(2)}) copy-start(bf16[1,256,2048]{2,1,0:T(8,128)(2,1)} %param.6) | copy-start | bytes 3145732
  6.5 119.6 %all-gather.2.cloned.1.call-start = ((), (), s32[]{:S(2)}) async-start(), calls=%async_computation.3 | async-start | bytes 1179648 | tf_op jit(solution)/shard_map/all_gather | solution.py:32
  41.4 0.7 copy-start.1
  42.3 0.7 copy-start.2
  43.8 85.0 %all-to-all-start.2 = ((s32[64,1,8]{2,1,0:T(1,128)}), s32[64,1,8]{2,1,0:T(1,128)S(1)}, u32[]{:S(2)}, u32[]{:S(2)}) async-start(s32[64,1,8]{2,1,0:T(1,128)} %bitcast.6), calls=%async_computation.2 | async-start | bytes 65536 | tf_op jit(solution)/shard_map/all_to_all | solution.py:26
  128.8 26.5 %all-to-all-start.1 = ((bf16[64,8,256]{2,1,0:T(8,128)(2,1)}), bf16[64,8,256]{2,1,0:T(8,128)(2,1)S(1)}, u32[]{:S(2)}, u32[]{:S(2)}) async-start(bf16[64,8,256]{2,1,0:T(8,128)(2,1)} %fusion.1), calls=%async_computation.1 | async-start | bytes 524288 | tf_op jit(solution)/shard_map/all_to_all | solution.py:38
  137.4 17.9 %copy-start.3 = (f32[1,256]{1,0:T(1,128)S(1)}, f32[1,256]{1,0:T(1,128)}, u32[]{:S(2)}) copy-start(f32[1,256]{1,0:T(1,128)} %param.9) | copy-start | bytes 3076
Sparse Core Ops, SparseCore 0:
  41.5 84.5 all-gather.1
